TPU v7x, 512 devices: a whole 4x8x8 slice. The times are simulated.
512 devices in a mesh: gs: 128 (over y, z, core), view: 4 (over x).
Axes of the slice: x: 4, y: 8, z: 8, core: 2. Of those that a mesh axis runs over, the one named last changes fastest.
Arguments:
- features: bfloat16 [131072, 128], P('gs'), may hold values from -6 to 6
- geometry: float32 [4, 9, 131072], P('view', None, 'gs'), as said below
- decoder: bfloat16 [128, 512], replicated, may hold values from -0.5 to 0.5
- teacher: bfloat16 [4, 131072, 512], P('view', 'gs'), may hold values from -3 to 3
- images: float32 [4, 3, 131072], P('view', None, 'gs'), may hold values from 0 to 1
- send_index: int32 [4, 128, 1024], P('view', 'gs'), may hold values from 0 to 1023, as said below
- tile_lists: int32 [4, 512, 8], P('view', 'gs'), may hold values from 0 to 7, as said below
- tile_lengths: int32 [4, 512], P('view', 'gs'), may hold values from 2 to 8
Outputs:
- feature_grad: float32 [131072, 128], P(('gs', 'view'))
- geometry_grad: float32 [4, 9, 131072], P('view', None, 'gs')
- decoder_grad: float32 [128, 512], replicated
Inputs may be any that keep to these rules, and one draw needn't show every extreme that they name: `send_index`: each row (one view, one source device) is a permutation of 0 .. 1023; positions k * 8 to (k + 1) * 8 - 1 hold the Gaussians sent to the device of gs index k. `tile_lists`: the 8 entries of a row are distinct. `geometry`: opacity logits lie in -7.5 .. -4, log conics between -2 log 16 and -2 log 16 + 2 log 4, shears in -2 .. 2, colors in 0 .. 1.
All inputs are finite; a program needn't handle non-finite values.
Results may differ from a plain program's by a relative error of at most 0.0017.
Values may be sent and summed in bfloat16 or wider, within the bound.
A program may use at most 64 MiB of HBM per device.

v0:
```python
import math
import jax
import jax.numpy as jnp
from jax import lax
from jax.sharding import PartitionSpec as P

FEAT = 128
CT = 512
TS = 16
BLK = 128
LIST = 8


def composite(tile_geo, alive_mask, pixel_x, pixel_y):
    delta_x = pixel_x[:, None] - tile_geo[0][None, :]
    delta_y = pixel_y[:, None] - tile_geo[1][None, :]
    conic_a = jnp.exp(tile_geo[2])
    conic_c = jnp.exp(tile_geo[3])
    conic_b = 0.8 * jnp.tanh(tile_geo[4]) * jnp.exp(0.5 * (tile_geo[2] + tile_geo[3]))
    exponent = -0.5 * (
        conic_a * delta_x * delta_x
        + 2.0 * conic_b * delta_x * delta_y
        + conic_c * delta_y * delta_y
    )
    opacity = alive_mask * jax.nn.sigmoid(tile_geo[5])
    alpha_val = opacity[None, :] * jnp.exp(exponent)
    log_keep = jnp.log1p(-alpha_val)
    pixel_count = pixel_x.shape[0]
    blocked = log_keep.reshape(pixel_count, LIST, BLK)
    inner = jnp.cumsum(blocked, axis=2) - blocked
    block_sums = jnp.sum(blocked, axis=2)
    outer = jnp.cumsum(block_sums, axis=1) - block_sums
    before = (inner + outer[:, :, None]).reshape(pixel_count, LIST * BLK)
    weights = alpha_val * jnp.exp(before)
    pixel_color = jnp.einsum("pi,ci->cp", weights, tile_geo[6:9], precision=lax.Precision.HIGHEST)
    return (weights, pixel_color)


def device_terms(
    recv_geo, recv_feat, decoder, teacher_dev, images_dev, lists, lengths, shard_index
):
    nblocks = recv_feat.shape[0] // BLK
    tile_pixels = TS * TS
    geo_blocks = recv_geo.reshape(9, nblocks, BLK)
    feat_blocks = recv_feat.reshape(nblocks, BLK, FEAT)
    within = jnp.arange(tile_pixels, dtype=jnp.int32)
    block_range = jnp.arange(nblocks, dtype=jnp.int32)
    slot_range = jnp.arange(LIST, dtype=jnp.int32)

    def tile_step(totals, tile_index):
        decoder_sum, geo_acc, feat_acc = totals
        block_ids = lists[tile_index]
        count = lengths[tile_index]
        alive_mask = jnp.broadcast_to(
            (slot_range < count).astype(jnp.float32)[:, None], (LIST, BLK)
        ).reshape(LIST * BLK)
        tile_geo = jnp.take(geo_blocks, block_ids, axis=1).reshape(9, LIST * BLK)
        feat_tile = jnp.take(feat_blocks, block_ids, axis=0).reshape(LIST * BLK, FEAT)
        column = 2 * TS * (shard_index % 30) + TS * (tile_index % 2) + within % TS
        row_index = 2 * TS * (shard_index // 30) + TS * (tile_index // 2) + within // TS
        pixel_x = column.astype(jnp.float32) + 0.5
        pixel_y = row_index.astype(jnp.float32) + 0.5
        (weights, pixel_color), pullback = jax.vjp(
            lambda geo_part: composite(geo_part, alive_mask, pixel_x, pixel_y), tile_geo
        )
        weight_b = weights.astype(jnp.bfloat16)
        rendered = jnp.dot(weight_b, feat_tile, preferred_element_type=jnp.float32).astype(
            jnp.bfloat16
        )
        pred = jnp.dot(rendered, decoder, preferred_element_type=jnp.float32)
        teacher_rows = lax.dynamic_slice_in_dim(
            teacher_dev, tile_index * tile_pixels, tile_pixels, 0
        )
        error_feat = pred - teacher_rows.astype(jnp.float32)
        gpred = (error_feat / jnp.sqrt(error_feat * error_feat + 0.04)).astype(jnp.bfloat16)
        grender = lax.dot_general(
            gpred, decoder, (((1,), (1,)), ((), ())), preferred_element_type=jnp.float32
        ).astype(jnp.bfloat16)
        decoder_sum = decoder_sum + lax.dot_general(
            rendered, gpred, (((0,), (0,)), ((), ())), preferred_element_type=jnp.float32
        )
        image_cols = lax.dynamic_slice_in_dim(images_dev, tile_index * tile_pixels, tile_pixels, 1)
        error_color = pixel_color - image_cols
        gcolor = error_color / jnp.sqrt(error_color * error_color + 0.04)
        gweight = lax.dot_general(
            grender, feat_tile, (((1,), (1,)), ((), ())), preferred_element_type=jnp.float32
        )
        gfeat_tile = lax.dot_general(
            weight_b, grender, (((0,), (0,)), ((), ())), preferred_element_type=jnp.float32
        )
        (ggeo_tile,) = pullback((gweight, gcolor))
        hits = (block_ids[:, None] == block_range[None, :]).astype(jnp.float32)
        geo_acc = geo_acc + jnp.einsum(
            "clb,ln->cnb", ggeo_tile.reshape(9, LIST, BLK), hits, precision=lax.Precision.HIGHEST
        )
        feat_acc = feat_acc + jnp.einsum(
            "ln,lbf->nbf",
            hits,
            gfeat_tile.reshape(LIST, BLK, FEAT),
            precision=lax.Precision.HIGHEST,
        )
        return ((decoder_sum, geo_acc, feat_acc), None)

    start_totals = (
        jnp.zeros((FEAT, CT), jnp.float32),
        jnp.zeros((9, nblocks, BLK), jnp.float32),
        jnp.zeros((nblocks, BLK, FEAT), jnp.float32),
    )
    tile_range = jnp.arange(lists.shape[0], dtype=jnp.int32)
    (decoder_sum, geo_acc, feat_acc), _ = lax.scan(tile_step, start_totals, tile_range)
    return (decoder_sum, geo_acc.reshape(9, nblocks * BLK), feat_acc.reshape(nblocks * BLK, FEAT))


def on_device(features, geometry, decoder, teacher, images, send_index, tile_lists, tile_lengths):
    send_order = send_index[0, 0]
    shard_index = lax.axis_index("gs")
    geo_send = jnp.take(geometry[0], send_order, axis=1)
    recv_geo = lax.all_to_all(geo_send, "gs", split_axis=1, concat_axis=1, tiled=True)
    feat_send = jnp.take(features, send_order, axis=0)
    recv_feat = lax.all_to_all(feat_send, "gs", split_axis=0, concat_axis=0, tiled=True)
    decoder_sum, geo_acc, feat_acc = device_terms(
        recv_geo,
        recv_feat,
        decoder,
        teacher[0],
        images[0],
        tile_lists[0],
        tile_lengths[0],
        shard_index,
    )
    returned_geo = lax.all_to_all(geo_acc, "gs", split_axis=1, concat_axis=1, tiled=True)
    returned_feat = lax.all_to_all(feat_acc, "gs", split_axis=0, concat_axis=0, tiled=True)
    geo_own = jnp.zeros_like(returned_geo).at[:, send_order].set(returned_geo)
    feat_own = jnp.zeros_like(returned_feat).at[send_order].set(returned_feat)
    quarter = feat_own.shape[0] // lax.axis_size("view")
    summed = lax.psum(feat_own, "view")
    feature_grad = lax.dynamic_slice_in_dim(summed, lax.axis_index("view") * quarter, quarter, 0)
    pixel_total = lax.axis_size("gs") * lax.axis_size("view") * tile_lists.shape[1] * TS * TS
    decoder_grad = lax.psum(decoder_sum, ("gs", "view")) * (1.0 / math.sqrt(pixel_total))
    return (feature_grad, geo_own[None], decoder_grad)


def solution(mesh):
    placed = (
        P("gs", None),
        P("view", None, "gs"),
        P(),
        P("view", "gs", None),
        P("view", None, "gs"),
        P("view", "gs", None),
        P("view", "gs", None),
        P("view", "gs"),
    )
    return jax.shard_map(
        on_device,
        mesh=mesh,
        in_specs=placed,
        out_specs=(P(("gs", "view"), None), P("view", None, "gs"), P()),
        check_vma=False,
    )
```

profile of v0, /device:TPU:8, one launch (start us, length us, event | category | flops | bytes accessed | tf_op | source)
XLA Modules:
  0.0 610.4 jit_solution(10011325874883574381)
XLA Ops:
  10.2 2.8 gather_fusion.2
  14.1 17.4 %all-to-all-start = ((f32[9,128,8]{0,2,1:T(8,128)}), f32[9,128,8]{0,2,1:T(8,128)S(1)}, u32[]{:S(2)}, u32[]{:S(2)}) async-start(f32[9,128,8]{0,2,1:T(8,128)} %bitcast_select_fusion.1), calls=%async_computation | async-start | bytes 1048576 | tf_op jit(solution)/shard_map/all_to_all | solution.py:118
  31.5 3.2 gather_fusion.3
  35.6 16.2 %all-to-all-done = f32[9,128,8]{0,2,1:T(8,128)S(1)} async-done(((f32[9,128,8]{0,2,1:T(8,128)}), f32[9,128,8]{0,2,1:T(8,128)S(1)}, u32[]{:S(2)}, u32[]{:S(2)}) %all-to-all-start) | async-done | bytes 36896 | tf_op jit(solution)/shard_map/all_to_all | solution.py:118
  51.8 6.5 %all-to-all-start.1 = ((bf16[128,8,128]{2,1,0:T(8,128)(2,1)}), bf16[128,8,128]{2,1,0:T(8,128)(2,1)S(1)}, u32[]{:S(2)}, u32[]{:S(2)}) async-start(bf16[128,8,128]{2,1,0:T(8,128)(2,1)} %bitcast_select_fusion.2), calls=%async_computation.1 | async-start | bytes 524288 | tf_op jit(solution)/shard_map/all_to_all | solution.py:120
  60.4 12.6 %all-to-all-done.1 = bf16[128,8,128]{2,1,0:T(8,128)(2,1)S(1)} async-done(((bf16[128,8,128]{2,1,0:T(8,128)(2,1)}), bf16[128,8,128]{2,1,0:T(8,128)(2,1)S(1)}, u32[]{:S(2)}, u32[]{:S(2)}) %all-to-all-start.1) | async-done | bytes 262176 | tf_op jit(solution)/shard_map/all_to_all | solution.py:120
  73.7 187.1 %while.21 = (s32[]{:T(128)}, f32[128,512]{1,0:T(8,128)}, f32[9,8,128]{2,1,0:T(8,128)}, f32[8,128,128]{2,0,1:T(8,128)}, s32[4]{0:T(128)S(1)}, /*index=5*/s32[4]{0...) while((s32[]{:T(128)}, f32[128,512]{1,0:T(8,128)}, ...), condition=%wide.region_13.14_spmd.clone.clone, body=%wide.region_0.13_spmd.clone.clone.sunk | while | flops 448201472 | bytes 62394652 | solution.py:110
  82.8 1.4 gather_fusion
  89.3 2.2 exponential_multiply_fusion.2
  91.6 1.1 fusion.164
  93.2 1.2 convert_bitcast_fusion.2
  95.6 1.4 rsqrt_multiply_fusion.2
  97.1 1.8 fusion.171
  98.9 1.2 multiply_convert_fusion.2
  101.7 1.2 convolution_add_fusion.8
  105.5 1.5 copy.140
  107.0 3.4 fusion.167
  110.4 1.5 copy.141
  114.7 2.3 fusion.168
  128.7 1.4 gather_fusion
  135.2 2.2 exponential_multiply_fusion.2
  137.5 1.1 fusion.164
  139.1 1.2 convert_bitcast_fusion.2
  141.6 1.4 rsqrt_multiply_fusion.2
  143.1 1.8 fusion.171
  144.9 1.2 multiply_convert_fusion.2
  147.6 2.3 convolution_add_fusion.8
  152.6 1.5 copy.140
  154.0 3.4 fusion.167
  157.4 1.5 copy.141
  161.7 2.3 fusion.168
  175.7 1.4 gather_fusion
  182.3 2.2 exponential_multiply_fusion.2
  186.2 1.2 convert_bitcast_fusion.2
  188.6 1.5 rsqrt_multiply_fusion.2
  190.1 1.8 fusion.171
  191.9 1.2 multiply_convert_fusion.2
  194.7 2.3 convolution_add_fusion.8
  199.6 1.5 copy.140
  201.1 3.4 fusion.167
  204.4 1.5 copy.141
  208.8 2.3 fusion.168
  222.8 1.4 gather_fusion
  229.3 2.2 exponential_multiply_fusion.2
  233.2 1.2 convert_bitcast_fusion.2
  235.6 1.5 rsqrt_multiply_fusion.2
  237.1 1.8 fusion.171
  239.0 1.2 multiply_convert_fusion.2
  241.7 2.3 convolution_add_fusion.8
  246.6 1.5 copy.140
  248.1 3.4 fusion.167
  251.5 1.5 copy.141
  255.8 2.3 fusion.168
  260.8 1.9 copy.80
  262.7 6.5 %all-to-all-start.2 = ((f32[128,8,128]{2,1,0:T(8,128)}), f32[128,8,128]{2,1,0:T(8,128)S(1)}, u32[]{:S(2)}, u32[]{:S(2)}) async-start(f32[128,8,128]{2,1,0:T(8,128)} %bitcast.11), calls=%async_computation.2 | async-start | bytes 1048576 | tf_op jit(solution)/shard_map/all_to_all | solution.py:132
  270.0 19.5 %all-to-all-done.2 = f32[128,8,128]{2,1,0:T(8,128)S(1)} async-done(((f32[128,8,128]{2,1,0:T(8,128)}), f32[128,8,128]{2,1,0:T(8,128)S(1)}, u32[]{:S(2)}, u32[]{:S(2)}) %all-to-all-start.2) | async-done | bytes 524320 | tf_op jit(solution)/shard_map/all_to_all | solution.py:132
  289.5 4.0 scatter_custom_fusion
  295.4 6.4 %all-to-all-start.3 = ((f32[9,128,8]{0,2,1:T(8,128)}), f32[9,128,8]{0,2,1:T(8,128)S(1)}, u32[]{:S(2)}, u32[]{:S(2)}) async-start(f32[9,128,8]{0,2,1:T(8,128)} %bitcast.13), calls=%async_computation.3 | async-start | bytes 1048576 | tf_op jit(solution)/shard_map/all_to_all | solution.py:131
  301.7 20.4 %all-to-all-done.3 = f32[9,128,8]{0,2,1:T(8,128)S(1)} async-done(((f32[9,128,8]{0,2,1:T(8,128)}), f32[9,128,8]{0,2,1:T(8,128)S(1)}, u32[]{:S(2)}, u32[]{:S(2)}) %all-to-all-start.3) | async-done | bytes 36896 | tf_op jit(solution)/shard_map/all_to_all | solution.py:131
  322.2 3.4 scatter_custom_fusion.1
  326.4 222.5 %all-reduce.14.cloned.1.call-done = f32[128,512]{1,0:T(8,128)} async-done(((f32[128,512]{1,0:T(8,128)}), f32[128,512]{1,0:T(8,128)}) %all-reduce.14.cloned.1.call-update) | async-done | bytes 262160 | tf_op jit(solution)/shard_map/psum | solution.py:139
  548.8 1.7 broadcast_multiply_fusion.2
  550.5 51.4 %all-reduce.12.cloned.1.call-done = f32[1024,128]{1,0:T(8,128)} async-done(((f32[1024,128]{1,0:T(8,128)}), f32[1024,128]{1,0:T(8,128)}) %all-reduce.12.cloned.1.call-update) | async-done | bytes 524304 | tf_op jit(solution)/shard_map/psum | solution.py:136
  602.0 1.6 constant_dynamic-slice_fusion.1
  (485 shorter events, 96.0 us)
Async XLA Ops:
  7.2 24.3 %copy-start = (bf16[1024,128]{1,0:T(8,128)(2,1)S(1)}, bf16[1024,128]{1,0:T(8,128)(2,1)}, u32[]{:S(2)}) copy-start(bf16[1024,128]{1,0:T(8,128)(2,1)} %param.10) | copy-start | bytes 786436
  14.1 37.7 %all-to-all-start = ((f32[9,128,8]{0,2,1:T(8,128)}), f32[9,128,8]{0,2,1:T(8,128)S(1)}, u32[]{:S(2)}, u32[]{:S(2)}) async-start(f32[9,128,8]{0,2,1:T(8,128)} %bitcast_select_fusion.1), calls=%async_computation | async-start | bytes 1048576 | tf_op jit(solution)/shard_map/all_to_all | solution.py:118
  51.8 21.3 %all-to-all-start.1 = ((bf16[128,8,128]{2,1,0:T(8,128)(2,1)}), bf16[128,8,128]{2,1,0:T(8,128)(2,1)S(1)}, u32[]{:S(2)}, u32[]{:S(2)}) async-start(bf16[128,8,128]{2,1,0:T(8,128)(2,1)} %bitcast_select_fusion.2), calls=%async_computation.1 | async-start | bytes 524288 | tf_op jit(solution)/shard_map/all_to_all | solution.py:120
  73.7 13.7 %copy-start.8 = (bf16[8,128,128]{2,1,0:T(8,128)(2,1)}, bf16[8,128,128]{2,1,0:T(8,128)(2,1)S(1)}, u32[]{:S(2)}) copy-start(bf16[8,128,128]{2,1,0:T(8,128)(2,1)S(1)} %get-tuple-element.843) | copy-start | bytes 786436 | tf_op jit(solution)/shard_map/while
  81.3 22.9 %copy-start.21 = (f32[256]{0:T(256)}, f32[256]{0:T(256)S(1)}, u32[]{:S(2)}) copy-start(f32[256]{0:T(256)S(1)} %get-tuple-element.768) | copy-start | bytes 3076 | tf_op jit(solution)/shard_map/while
  81.3 22.9 %copy-start.23 = (f32[256]{0:T(256)}, f32[256]{0:T(256)S(1)}, u32[]{:S(2)}) copy-start(f32[256]{0:T(256)S(1)} %get-tuple-element.765) | copy-start | bytes 3076 | tf_op jit(solution)/shard_map/while
  82.0 19.6 %copy-start.28 = (s32[8]{0:T(128)}, s32[8]{0:T(128)S(1)}, u32[]{:S(2)}) copy-start(s32[8]{0:T(128)S(1)} %get-tuple-element.785) | copy-start | bytes 100 | tf_op jit(solution)/shard_map/while
  84.2 18.9 %copy-start.5 = (f32[9,8,128]{2,0,1:T(8,128)}, f32[9,8,128]{2,0,1:T(8,128)S(1)}, u32[]{:S(2)}) copy-start(f32[9,8,128]{2,0,1:T(8,128)S(1)} %select_bitcast_fusion.2) | copy-start | bytes 110596 | tf_op jit(solution)/shard_map/while
  84.9 19.4 %copy-start.11 = (f32[1,8,128]{2,0,1:T(1,128)}, f32[1,8,128]{2,0,1:T(1,128)S(1)}, u32[]{:S(2)}) copy-start(f32[1,8,128]{2,0,1:T(1,128)S(1)} %get-tuple-element.769) | copy-start | bytes 12292 | tf_op jit(solution)/shard_map/while
  85.5 18.8 %copy-start.16 = (f32[1024]{0:T(1024)}, f32[1024]{0:T(1024)S(1)}, u32[]{:S(2)}) copy-start(f32[1024]{0:T(1024)S(1)} %bitcast_multiply_fusion.8) | copy-start | bytes 12292 | tf_op jit(solution)/shard_map/while
  111.9 2.1 copy-start.3
  114.7 2.3 copy-start.15
  114.7 2.3 copy-start.26
  114.7 2.4 copy-start.27
  114.7 3.3 copy-start.25
  117.0 2.6 copy-start.9
  119.6 13.7 %copy-start.8 = (bf16[8,128,128]{2,1,0:T(8,128)(2,1)}, bf16[8,128,128]{2,1,0:T(8,128)(2,1)S(1)}, u32[]{:S(2)}) copy-start(bf16[8,128,128]{2,1,0:T(8,128)(2,1)S(1)} %get-tuple-element.843) | copy-start | bytes 786436 | tf_op jit(solution)/shard_map/while
  127.3 24.0 %copy-start.21 = (f32[256]{0:T(256)}, f32[256]{0:T(256)S(1)}, u32[]{:S(2)}) copy-start(f32[256]{0:T(256)S(1)} %get-tuple-element.768) | copy-start | bytes 3076 | tf_op jit(solution)/shard_map/while
  127.3 24.0 %copy-start.23 = (f32[256]{0:T(256)}, f32[256]{0:T(256)S(1)}, u32[]{:S(2)}) copy-start(f32[256]{0:T(256)S(1)} %get-tuple-element.765) | copy-start | bytes 3076 | tf_op jit(solution)/shard_map/while
  128.0 19.6 %copy-start.28 = (s32[8]{0:T(128)}, s32[8]{0:T(128)S(1)}, u32[]{:S(2)}) copy-start(s32[8]{0:T(128)S(1)} %get-tuple-element.785) | copy-start | bytes 100 | tf_op jit(solution)/shard_map/while
  130.2 20.0 %copy-start.5 = (f32[9,8,128]{2,0,1:T(8,128)}, f32[9,8,128]{2,0,1:T(8,128)S(1)}, u32[]{:S(2)}) copy-start(f32[9,8,128]{2,0,1:T(8,128)S(1)} %select_bitcast_fusion.2) | copy-start | bytes 110596 | tf_op jit(solution)/shard_map/while
  130.8 20.5 %copy-start.11 = (f32[1,8,128]{2,0,1:T(1,128)}, f32[1,8,128]{2,0,1:T(1,128)S(1)}, u32[]{:S(2)}) copy-start(f32[1,8,128]{2,0,1:T(1,128)S(1)} %get-tuple-element.769) | copy-start | bytes 12292 | tf_op jit(solution)/shard_map/while
  131.4 19.9 %copy-start.16 = (f32[1024]{0:T(1024)}, f32[1024]{0:T(1024)S(1)}, u32[]{:S(2)}) copy-start(f32[1024]{0:T(1024)S(1)} %bitcast_multiply_fusion.8) | copy-start | bytes 12292 | tf_op jit(solution)/shard_map/while
  147.3 2.6 copy-start.7
  147.6 2.3 copy-start.4
  161.7 2.3 copy-start.15
  161.7 2.3 copy-start.26
  161.7 2.4 copy-start.27
  161.7 3.3 copy-start.25
  164.0 2.6 copy-start.9
  166.6 13.7 %copy-start.8 = (bf16[8,128,128]{2,1,0:T(8,128)(2,1)}, bf16[8,128,128]{2,1,0:T(8,128)(2,1)S(1)}, u32[]{:S(2)}) copy-start(bf16[8,128,128]{2,1,0:T(8,128)(2,1)S(1)} %get-tuple-element.843) | copy-start | bytes 786436 | tf_op jit(solution)/shard_map/while
  174.3 24.0 %copy-start.21 = (f32[256]{0:T(256)}, f32[256]{0:T(256)S(1)}, u32[]{:S(2)}) copy-start(f32[256]{0:T(256)S(1)} %get-tuple-element.768) | copy-start | bytes 3076 | tf_op jit(solution)/shard_map/while
  174.3 24.0 %copy-start.23 = (f32[256]{0:T(256)}, f32[256]{0:T(256)S(1)}, u32[]{:S(2)}) copy-start(f32[256]{0:T(256)S(1)} %get-tuple-element.765) | copy-start | bytes 3076 | tf_op jit(solution)/shard_map/while
  175.0 19.6 %copy-start.28 = (s32[8]{0:T(128)}, s32[8]{0:T(128)S(1)}, u32[]{:S(2)}) copy-start(s32[8]{0:T(128)S(1)} %get-tuple-element.785) | copy-start | bytes 100 | tf_op jit(solution)/shard_map/while
  177.2 20.0 %copy-start.5 = (f32[9,8,128]{2,0,1:T(8,128)}, f32[9,8,128]{2,0,1:T(8,128)S(1)}, u32[]{:S(2)}) copy-start(f32[9,8,128]{2,0,1:T(8,128)S(1)} %select_bitcast_fusion.2) | copy-start | bytes 110596 | tf_op jit(solution)/shard_map/while
  177.8 20.5 %copy-start.11 = (f32[1,8,128]{2,0,1:T(1,128)}, f32[1,8,128]{2,0,1:T(1,128)S(1)}, u32[]{:S(2)}) copy-start(f32[1,8,128]{2,0,1:T(1,128)S(1)} %get-tuple-element.769) | copy-start | bytes 12292 | tf_op jit(solution)/shard_map/while
  178.4 19.9 %copy-start.16 = (f32[1024]{0:T(1024)}, f32[1024]{0:T(1024)S(1)}, u32[]{:S(2)}) copy-start(f32[1024]{0:T(1024)S(1)} %bitcast_multiply_fusion.8) | copy-start | bytes 12292 | tf_op jit(solution)/shard_map/while
  194.3 2.6 copy-start.7
  194.6 2.3 copy-start.4
  205.9 2.1 copy-start.3
  208.7 2.3 copy-start.15
  208.7 2.3 copy-start.26
  208.7 2.4 copy-start.27
  208.7 3.3 copy-start.25
  211.0 2.6 copy-start.9
  213.7 13.7 %copy-start.8 = (bf16[8,128,128]{2,1,0:T(8,128)(2,1)}, bf16[8,128,128]{2,1,0:T(8,128)(2,1)S(1)}, u32[]{:S(2)}) copy-start(bf16[8,128,128]{2,1,0:T(8,128)(2,1)S(1)} %get-tuple-element.843) | copy-start | bytes 786436 | tf_op jit(solution)/shard_map/while
  221.3 24.0 %copy-start.21 = (f32[256]{0:T(256)}, f32[256]{0:T(256)S(1)}, u32[]{:S(2)}) copy-start(f32[256]{0:T(256)S(1)} %get-tuple-element.768) | copy-start | bytes 3076 | tf_op jit(solution)/shard_map/while
  221.3 24.0 %copy-start.23 = (f32[256]{0:T(256)}, f32[256]{0:T(256)S(1)}, u32[]{:S(2)}) copy-start(f32[256]{0:T(256)S(1)} %get-tuple-element.765) | copy-start | bytes 3076 | tf_op jit(solution)/shard_map/while
  222.0 19.6 %copy-start.28 = (s32[8]{0:T(128)}, s32[8]{0:T(128)S(1)}, u32[]{:S(2)}) copy-start(s32[8]{0:T(128)S(1)} %get-tuple-element.785) | copy-start | bytes 100 | tf_op jit(solution)/shard_map/while
  224.2 20.0 %copy-start.5 = (f32[9,8,128]{2,0,1:T(8,128)}, f32[9,8,128]{2,0,1:T(8,128)S(1)}, u32[]{:S(2)}) copy-start(f32[9,8,128]{2,0,1:T(8,128)S(1)} %select_bitcast_fusion.2) | copy-start | bytes 110596 | tf_op jit(solution)/shard_map/while
  224.9 20.5 %copy-start.11 = (f32[1,8,128]{2,0,1:T(1,128)}, f32[1,8,128]{2,0,1:T(1,128)S(1)}, u32[]{:S(2)}) copy-start(f32[1,8,128]{2,0,1:T(1,128)S(1)} %get-tuple-element.769) | copy-start | bytes 12292 | tf_op jit(solution)/shard_map/while
  225.5 19.9 %copy-start.16 = (f32[1024]{0:T(1024)}, f32[1024]{0:T(1024)S(1)}, u32[]{:S(2)}) copy-start(f32[1024]{0:T(1024)S(1)} %bitcast_multiply_fusion.8) | copy-start | bytes 12292 | tf_op jit(solution)/shard_map/while
  241.4 2.6 copy-start.7
  241.7 2.3 copy-start.4
  253.0 2.1 copy-start.3
  255.8 2.3 copy-start.15
  255.8 2.3 copy-start.26
  255.8 2.4 copy-start.27
  255.8 3.3 copy-start.25
  258.1 2.6 copy-start.9
  262.7 26.8 %all-to-all-start.2 = ((f32[128,8,128]{2,1,0:T(8,128)}), f32[128,8,128]{2,1,0:T(8,128)S(1)}, u32[]{:S(2)}, u32[]{:S(2)}) async-start(f32[128,8,128]{2,1,0:T(8,128)} %bitcast.11), calls=%async_computation.2 | async-start | bytes 1048576 | tf_op jit(solution)/shard_map/all_to_all | solution.py:132
  269.2 279.6 %all-reduce.14.cloned.1.call-start = ((), (), s32[]{:S(2)}) async-start(), calls=%async_computation.5 | async-start | bytes 524288 | tf_op jit(solution)/shard_map/psum | solution.py:139
  269.9 332.0 %all-reduce.12.cloned.1.call-start = ((), (), s32[]{:S(2)}) async-start(), calls=%async_computation.4 | async-start | bytes 1048576 | tf_op jit(solution)/shard_map/psum | solution.py:136
  295.4 26.8 %all-to-all-start.3 = ((f32[9,128,8]{0,2,1:T(8,128)}), f32[9,128,8]{0,2,1:T(8,128)S(1)}, u32[]{:S(2)}, u32[]{:S(2)}) async-start(f32[9,128,8]{0,2,1:T(8,128)} %bitcast.13), calls=%async_computation.3 | async-start | bytes 1048576 | tf_op jit(solution)/shard_map/all_to_all | solution.py:131
  (73 other events, 68.1 us)
Sparse Core Ops, SparseCore 0:
  275.6 273.1 all-reduce.13
  551.3 50.6 all-reduce.11
where the time goes:
time: 613 us; the launch traced here: 610 us
  waiting for transfers between devices  343 us (56%)
  local copies, waits for them, and re-layouts  79.9 us (13%)
  other arithmetic  76.6 us (12%)
  matrix products  39.1 us (6%)
  starting transfers between devices  36.8 us (6%)
  loops' own time  20.3 us (3%)
  between operations  14.3 us (2%)
    psum x1, waiting for transfers between devices, on_device(): lax.psum(decoder_sum, ('gs', 'view')) * (1.0 / math.sqrt(pixel_total))  222 us
    psum x1, waiting for transfers between devices, on_device(): summed = lax.psum(feat_own, 'view')  51.4 us
    another operation x8, other arithmetic, composite(): inner = jnp.cumsum(blocked, axis=2) - blocked  22.4 us
    all_to_all x1, waiting for transfers between devices, on_device(): lax.all_to_all(geo_acc, 'gs', split_axis=1, concat_axis=1, tiled=True)  20.4 us
    another operation x1, loops' own time, device_terms(): lax.scan(tile_step, start_totals, tile_range)  20.3 us
    all_to_all x1, waiting for transfers between devices, on_device(): lax.all_to_all(feat_acc, 'gs', split_axis=0, concat_axis=0, tiled=True)  19.5 us
    while x264, local copies, waits for them, and re-layouts  19.3 us
    all_to_all x1, starting transfers between devices, on_device(): lax.all_to_all(geo_send, 'gs', split_axis=1, concat_axis=1, tiled=True)  17.4 us
  transfers between devices with their start and end apart: 6, of which 6 were waited for; matrix products, arithmetic and copies ran while one was open for 3% of the time, Pallas kernels for 0%

commit v1 on v0

--- a/solution.py
+++ b/solution.py
@@ -133,7 +133,7 @@
     geo_own = jnp.zeros_like(returned_geo).at[:, send_order].set(returned_geo)
     feat_own = jnp.zeros_like(returned_feat).at[send_order].set(returned_feat)
     quarter = feat_own.shape[0] // lax.axis_size("view")
-    summed = lax.psum(feat_own, "view")
+    summed = jnp.sum(jax.lax.all_gather(feat_own, "view"), axis=0)
     feature_grad = lax.dynamic_slice_in_dim(summed, lax.axis_index("view") * quarter, quarter, 0)
     pixel_total = lax.axis_size("gs") * lax.axis_size("view") * tile_lists.shape[1] * TS * TS
     decoder_grad = lax.psum(decoder_sum, ("gs", "view")) * (1.0 / math.sqrt(pixel_total))

time: 613 us -> 572 us (0.933)
  the two profiles are of different devices: /device:TPU:8 before, /device:TPU:23 now
where the time goes in v1:
time: 572 us; the launch traced here: 569 us
  waiting for transfers between devices  288 us (50%)
  other arithmetic  81.8 us (14%)
  local copies, waits for them, and re-layouts  74 us (13%)
  starting transfers between devices  44.8 us (8%)
  matrix products  44.6 us (8%)
  loops' own time  20.1 us (4%)
  between operations  15.7 us (3%)
    psum x1, waiting for transfers between devices, on_device(): lax.psum(decoder_sum, ('gs', 'view')) * (1.0 / math.sqrt(pixel_total))  227 us
    another operation x8, other arithmetic, composite(): inner = jnp.cumsum(blocked, axis=2) - blocked  22.4 us
    another operation x1, loops' own time, device_terms(): lax.scan(tile_step, start_totals, tile_range)  20.1 us
    all_to_all x1, waiting for transfers between devices, on_device(): lax.all_to_all(geo_acc, 'gs', split_axis=1, concat_axis=1, tiled=True)  18 us
    all_to_all x1, starting transfers between devices, on_device(): lax.all_to_all(geo_send, 'gs', split_axis=1, concat_axis=1, tiled=True)  17.8 us
    dot_general x12, matrix products, composite(): jnp.einsum('pi,ci->cp', weights, tile_geo[6:9], precision=lax.Precision.H...  17.3 us
    all_to_all x1, waiting for transfers between devices, on_device(): lax.all_to_all(feat_acc, 'gs', split_axis=0, concat_axis=0, tiled=True)  17.1 us
    all_to_all x1, waiting for transfers between devices, on_device(): lax.all_to_all(geo_send, 'gs', split_axis=1, concat_axis=1, tiled=True)  13.8 us
  transfers between devices with their start and end apart: 6, of which 5 were waited for; matrix products, arithmetic and copies ran while one was open for 3% of the time, Pallas kernels for 0%

profile of v1, /device:TPU:23, one launch (start us, length us, event | category | flops | bytes accessed | tf_op | source)
XLA Modules:
  0.0 569.2 jit_solution(16678067210179080570)
XLA Ops:
  9.3 1.3 reduce.5
  11.7 2.8 gather_fusion.2
  15.6 17.8 %all-to-all-start = ((f32[9,128,8]{0,2,1:T(8,128)}), f32[9,128,8]{0,2,1:T(8,128)S(1)}, u32[]{:S(2)}, u32[]{:S(2)}) async-start(f32[9,128,8]{0,2,1:T(8,128)} %bitcast_select_fusion.1), calls=%async_computation | async-start | bytes 1048576 | tf_op jit(solution)/shard_map/all_to_all | solution.py:118
  33.4 3.2 gather_fusion.3
  37.5 13.8 %all-to-all-done = f32[9,128,8]{0,2,1:T(8,128)S(1)} async-done(((f32[9,128,8]{0,2,1:T(8,128)}), f32[9,128,8]{0,2,1:T(8,128)S(1)}, u32[]{:S(2)}, u32[]{:S(2)}) %all-to-all-start) | async-done | bytes 36896 | tf_op jit(solution)/shard_map/all_to_all | solution.py:118
  51.3 9.9 %all-to-all-start.1 = ((bf16[128,8,128]{2,1,0:T(8,128)(2,1)}), bf16[128,8,128]{2,1,0:T(8,128)(2,1)}, u32[]{:S(2)}, u32[]{:S(2)}) async-start(bf16[128,8,128]{2,1,0:T(8,128)(2,1)} %bitcast_select_fusion.2), calls=%async_computation.1 | async-start | bytes 524288 | tf_op jit(solution)/shard_map/all_to_all | solution.py:120
  62.7 11.3 %all-to-all-done.1 = bf16[128,8,128]{2,1,0:T(8,128)(2,1)} async-done(((bf16[128,8,128]{2,1,0:T(8,128)(2,1)}), bf16[128,8,128]{2,1,0:T(8,128)(2,1)}, u32[]{:S(2)}, u32[]{:S(2)}) %all-to-all-start.1) | async-done | bytes 262176 | tf_op jit(solution)/shard_map/all_to_all | solution.py:120
  74.5 191.7 %while.21 = (s32[]{:T(128)}, f32[128,512]{1,0:T(8,128)}, f32[9,8,128]{2,1,0:T(8,128)}, f32[8,128,128]{2,0,1:T(8,128)}, s32[4]{0:T(128)}, /*index=5*/s32[4]{0:T(1...) while((s32[]{:T(128)}, f32[128,512]{1,0:T(8,128)}, ...), condition=%wide.region_13.14_spmd.clone.clone, body=%wide.region_0.13_spmd.clone.clone.sunk | while | flops 448201472 | bytes 58158880 | solution.py:110
  80.2 1.2 dynamic_slice.78
  84.3 1.4 gather_fusion
  88.4 1.6 gather_fusion.1
  91.3 2.2 exponential_multiply_fusion.2
  97.6 1.5 rsqrt_multiply_fusion.2
  99.1 1.8 fusion.171
  107.5 1.5 copy.161
  109.0 3.4 fusion.167
  112.4 1.5 copy.162
  116.1 3.0 fusion.168
  126.7 1.2 dynamic_slice.78
  130.8 1.4 gather_fusion
  134.9 1.6 gather_fusion.1
  137.8 2.2 exponential_multiply_fusion.2
  144.1 1.4 rsqrt_multiply_fusion.2
  145.6 1.8 fusion.171
  148.9 1.9 convolution_add_fusion.6
  151.0 2.2 convolution_add_fusion.8
  155.9 1.5 copy.161
  157.4 3.4 fusion.167
  160.8 1.5 copy.162
  164.5 3.0 fusion.168
  175.1 1.2 dynamic_slice.78
  179.2 1.4 gather_fusion
  183.3 1.6 gather_fusion.1
  186.2 2.2 exponential_multiply_fusion.2
  192.5 1.5 rsqrt_multiply_fusion.2
  194.0 1.8 fusion.171
  197.3 1.9 convolution_add_fusion.6
  199.5 2.2 convolution_add_fusion.8
  204.4 1.5 copy.161
  205.9 3.4 fusion.167
  209.2 1.5 copy.162
  212.9 3.0 fusion.168
  223.5 1.2 dynamic_slice.78
  227.6 1.4 gather_fusion
  231.7 1.6 gather_fusion.1
  234.6 2.2 exponential_multiply_fusion.2
  240.9 1.4 rsqrt_multiply_fusion.2
  242.4 1.8 fusion.171
  245.7 1.9 convolution_add_fusion.6
  247.9 2.2 convolution_add_fusion.8
  252.8 1.5 copy.161
  254.3 3.4 fusion.167
  257.7 1.5 copy.162
  261.3 3.0 fusion.168
  266.2 1.9 copy.101
  268.2 8.1 %all-to-all-start.2 = ((f32[128,8,128]{2,1,0:T(8,128)}), f32[128,8,128]{2,1,0:T(8,128)S(1)}, u32[]{:S(2)}, u32[]{:S(2)}) async-start(f32[128,8,128]{2,1,0:T(8,128)} %bitcast.11), calls=%async_computation.2 | async-start | bytes 1048576 | tf_op jit(solution)/shard_map/all_to_all | solution.py:132
  277.1 17.1 %all-to-all-done.2 = f32[128,8,128]{2,1,0:T(8,128)S(1)} async-done(((f32[128,8,128]{2,1,0:T(8,128)}), f32[128,8,128]{2,1,0:T(8,128)S(1)}, u32[]{:S(2)}, u32[]{:S(2)}) %all-to-all-start.2) | async-done | bytes 524320 | tf_op jit(solution)/shard_map/all_to_all | solution.py:132
  294.2 4.0 scatter_custom_fusion
  299.3 8.8 %all-to-all-start.3 = ((f32[9,128,8]{0,2,1:T(8,128)}), f32[9,128,8]{0,2,1:T(8,128)S(1)}, u32[]{:S(2)}, u32[]{:S(2)}) async-start(f32[9,128,8]{0,2,1:T(8,128)} %bitcast.14), calls=%async_computation.3 | async-start | bytes 1048576 | tf_op jit(solution)/shard_map/all_to_all | solution.py:131
  308.1 18.0 %all-to-all-done.3 = f32[9,128,8]{0,2,1:T(8,128)S(1)} async-done(((f32[9,128,8]{0,2,1:T(8,128)}), f32[9,128,8]{0,2,1:T(8,128)S(1)}, u32[]{:S(2)}, u32[]{:S(2)}) %all-to-all-start.3) | async-done | bytes 36896 | tf_op jit(solution)/shard_map/all_to_all | solution.py:131
  326.1 3.4 scatter_custom_fusion.1
  330.3 227.4 %all-reduce.11.cloned.1.call-done = f32[128,512]{1,0:T(8,128)} async-done(((f32[128,512]{1,0:T(8,128)}), f32[128,512]{1,0:T(8,128)}) %all-reduce.11.cloned.1.call-update) | async-done | bytes 262160 | tf_op jit(solution)/shard_map/psum | solution.py:139
  557.7 1.7 broadcast_multiply_fusion.2
  559.4 1.8 reduce_sum.170
  (392 shorter events, 92.6 us)
Async XLA Ops:
  8.0 25.4 %copy-start = (bf16[1024,128]{1,0:T(8,128)(2,1)S(1)}, bf16[1024,128]{1,0:T(8,128)(2,1)}, u32[]{:S(2)}) copy-start(bf16[1024,128]{1,0:T(8,128)(2,1)} %param.10) | copy-start | bytes 786436
  15.6 45.7 %copy-start.23 = (f32[1,3,1024]{2,0,1:T(1,128)S(1)}, f32[1,3,1024]{2,0,1:T(1,128)}, u32[]{:S(2)}) copy-start(f32[1,3,1024]{2,0,1:T(1,128)} %param.14) | copy-start | bytes 36868
  15.6 35.7 %all-to-all-start = ((f32[9,128,8]{0,2,1:T(8,128)}), f32[9,128,8]{0,2,1:T(8,128)S(1)}, u32[]{:S(2)}, u32[]{:S(2)}) async-start(f32[9,128,8]{0,2,1:T(8,128)} %bitcast_select_fusion.1), calls=%async_computation | async-start | bytes 1048576 | tf_op jit(solution)/shard_map/all_to_all | solution.py:118
  51.3 22.7 %all-to-all-start.1 = ((bf16[128,8,128]{2,1,0:T(8,128)(2,1)}), bf16[128,8,128]{2,1,0:T(8,128)(2,1)}, u32[]{:S(2)}, u32[]{:S(2)}) async-start(bf16[128,8,128]{2,1,0:T(8,128)(2,1)} %bitcast_select_fusion.2), calls=%async_computation.1 | async-start | bytes 524288 | tf_op jit(solution)/shard_map/all_to_all | solution.py:120
  82.9 23.4 %copy-start.15 = (f32[256]{0:T(256)}, f32[256]{0:T(256)S(1)}, u32[]{:S(2)}) copy-start(f32[256]{0:T(256)S(1)} %get-tuple-element.785) | copy-start | bytes 3076 | tf_op jit(solution)/shard_map/while
  82.9 23.4 %copy-start.16 = (f32[256]{0:T(256)}, f32[256]{0:T(256)S(1)}, u32[]{:S(2)}) copy-start(f32[256]{0:T(256)S(1)} %get-tuple-element.782) | copy-start | bytes 3076 | tf_op jit(solution)/shard_map/while
  83.6 20.1 %copy-start.20 = (s32[8]{0:T(128)}, s32[8]{0:T(128)S(1)}, u32[]{:S(2)}) copy-start(s32[8]{0:T(128)S(1)} %get-tuple-element.802) | copy-start | bytes 100 | tf_op jit(solution)/shard_map/while
  85.8 19.4 %copy-start.5 = (f32[9,8,128]{2,0,1:T(8,128)}, f32[9,8,128]{2,0,1:T(8,128)S(1)}, u32[]{:S(2)}) copy-start(f32[9,8,128]{2,0,1:T(8,128)S(1)} %select_bitcast_fusion.2) | copy-start | bytes 110596 | tf_op jit(solution)/shard_map/while
  86.4 19.8 %copy-start.7 = (f32[1,8,128]{2,0,1:T(1,128)}, f32[1,8,128]{2,0,1:T(1,128)S(1)}, u32[]{:S(2)}) copy-start(f32[1,8,128]{2,0,1:T(1,128)S(1)} %get-tuple-element.786) | copy-start | bytes 12292 | tf_op jit(solution)/shard_map/while
  86.5 19.8 %copy-start.11 = (f32[1024]{0:T(1024)}, f32[1024]{0:T(1024)S(1)}, u32[]{:S(2)}) copy-start(f32[1024]{0:T(1024)S(1)} %bitcast_multiply_fusion.8) | copy-start | bytes 12292 | tf_op jit(solution)/shard_map/while
  102.2 2.7 copy-start.4
  113.9 2.1 copy-start.3
  116.0 3.1 copy-start.10
  116.0 3.1 copy-start.18
  116.0 3.1 copy-start.19
  116.0 4.0 copy-start.17
  116.0 4.1 copy-start.12
  116.1 4.1 copy-start.21
  129.3 25.3 %copy-start.15 = (f32[256]{0:T(256)}, f32[256]{0:T(256)S(1)}, u32[]{:S(2)}) copy-start(f32[256]{0:T(256)S(1)} %get-tuple-element.785) | copy-start | bytes 3076 | tf_op jit(solution)/shard_map/while
  129.3 25.3 %copy-start.16 = (f32[256]{0:T(256)}, f32[256]{0:T(256)S(1)}, u32[]{:S(2)}) copy-start(f32[256]{0:T(256)S(1)} %get-tuple-element.782) | copy-start | bytes 3076 | tf_op jit(solution)/shard_map/while
  130.0 21.0 %copy-start.20 = (s32[8]{0:T(128)}, s32[8]{0:T(128)S(1)}, u32[]{:S(2)}) copy-start(s32[8]{0:T(128)S(1)} %get-tuple-element.802) | copy-start | bytes 100 | tf_op jit(solution)/shard_map/while
  132.3 21.3 %copy-start.5 = (f32[9,8,128]{2,0,1:T(8,128)}, f32[9,8,128]{2,0,1:T(8,128)S(1)}, u32[]{:S(2)}) copy-start(f32[9,8,128]{2,0,1:T(8,128)S(1)} %select_bitcast_fusion.2) | copy-start | bytes 110596 | tf_op jit(solution)/shard_map/while
  132.9 21.8 %copy-start.7 = (f32[1,8,128]{2,0,1:T(1,128)}, f32[1,8,128]{2,0,1:T(1,128)S(1)}, u32[]{:S(2)}) copy-start(f32[1,8,128]{2,0,1:T(1,128)S(1)} %get-tuple-element.786) | copy-start | bytes 12292 | tf_op jit(solution)/shard_map/while
  133.0 21.7 %copy-start.11 = (f32[1024]{0:T(1024)}, f32[1024]{0:T(1024)S(1)}, u32[]{:S(2)}) copy-start(f32[1024]{0:T(1024)S(1)} %bitcast_multiply_fusion.8) | copy-start | bytes 12292 | tf_op jit(solution)/shard_map/while
  148.6 4.7 copy-start.4
  162.3 2.1 copy-start.3
  164.4 3.1 copy-start.10
  164.4 3.1 copy-start.18
  164.4 3.1 copy-start.19
  164.5 4.0 copy-start.17
  164.5 4.1 copy-start.12
  164.5 4.1 copy-start.21
  177.7 25.3 %copy-start.15 = (f32[256]{0:T(256)}, f32[256]{0:T(256)S(1)}, u32[]{:S(2)}) copy-start(f32[256]{0:T(256)S(1)} %get-tuple-element.785) | copy-start | bytes 3076 | tf_op jit(solution)/shard_map/while
  177.7 25.3 %copy-start.16 = (f32[256]{0:T(256)}, f32[256]{0:T(256)S(1)}, u32[]{:S(2)}) copy-start(f32[256]{0:T(256)S(1)} %get-tuple-element.782) | copy-start | bytes 3076 | tf_op jit(solution)/shard_map/while
  178.5 21.0 %copy-start.20 = (s32[8]{0:T(128)}, s32[8]{0:T(128)S(1)}, u32[]{:S(2)}) copy-start(s32[8]{0:T(128)S(1)} %get-tuple-element.802) | copy-start | bytes 100 | tf_op jit(solution)/shard_map/while
  180.7 21.3 %copy-start.5 = (f32[9,8,128]{2,0,1:T(8,128)}, f32[9,8,128]{2,0,1:T(8,128)S(1)}, u32[]{:S(2)}) copy-start(f32[9,8,128]{2,0,1:T(8,128)S(1)} %select_bitcast_fusion.2) | copy-start | bytes 110596 | tf_op jit(solution)/shard_map/while
  181.3 21.8 %copy-start.7 = (f32[1,8,128]{2,0,1:T(1,128)}, f32[1,8,128]{2,0,1:T(1,128)S(1)}, u32[]{:S(2)}) copy-start(f32[1,8,128]{2,0,1:T(1,128)S(1)} %get-tuple-element.786) | copy-start | bytes 12292 | tf_op jit(solution)/shard_map/while
  181.4 21.7 %copy-start.11 = (f32[1024]{0:T(1024)}, f32[1024]{0:T(1024)S(1)}, u32[]{:S(2)}) copy-start(f32[1024]{0:T(1024)S(1)} %bitcast_multiply_fusion.8) | copy-start | bytes 12292 | tf_op jit(solution)/shard_map/while
  197.0 4.7 copy-start.4
  212.8 3.1 copy-start.10
  212.9 3.1 copy-start.18
  212.9 3.1 copy-start.19
  212.9 4.0 copy-start.17
  212.9 4.1 copy-start.12
  212.9 4.1 copy-start.21
  226.2 25.3 %copy-start.15 = (f32[256]{0:T(256)}, f32[256]{0:T(256)S(1)}, u32[]{:S(2)}) copy-start(f32[256]{0:T(256)S(1)} %get-tuple-element.785) | copy-start | bytes 3076 | tf_op jit(solution)/shard_map/while
  226.2 25.3 %copy-start.16 = (f32[256]{0:T(256)}, f32[256]{0:T(256)S(1)}, u32[]{:S(2)}) copy-start(f32[256]{0:T(256)S(1)} %get-tuple-element.782) | copy-start | bytes 3076 | tf_op jit(solution)/shard_map/while
  226.9 21.0 %copy-start.20 = (s32[8]{0:T(128)}, s32[8]{0:T(128)S(1)}, u32[]{:S(2)}) copy-start(s32[8]{0:T(128)S(1)} %get-tuple-element.802) | copy-start | bytes 100 | tf_op jit(solution)/shard_map/while
  229.1 21.3 %copy-start.5 = (f32[9,8,128]{2,0,1:T(8,128)}, f32[9,8,128]{2,0,1:T(8,128)S(1)}, u32[]{:S(2)}) copy-start(f32[9,8,128]{2,0,1:T(8,128)S(1)} %select_bitcast_fusion.2) | copy-start | bytes 110596 | tf_op jit(solution)/shard_map/while
  229.7 21.8 %copy-start.7 = (f32[1,8,128]{2,0,1:T(1,128)}, f32[1,8,128]{2,0,1:T(1,128)S(1)}, u32[]{:S(2)}) copy-start(f32[1,8,128]{2,0,1:T(1,128)S(1)} %get-tuple-element.786) | copy-start | bytes 12292 | tf_op jit(solution)/shard_map/while
  229.8 21.7 %copy-start.11 = (f32[1024]{0:T(1024)}, f32[1024]{0:T(1024)S(1)}, u32[]{:S(2)}) copy-start(f32[1024]{0:T(1024)S(1)} %bitcast_multiply_fusion.8) | copy-start | bytes 12292 | tf_op jit(solution)/shard_map/while
  245.5 4.7 copy-start.4
  259.2 2.1 copy-start.3
  261.3 3.1 copy-start.10
  261.3 3.1 copy-start.18
  261.3 3.1 copy-start.19
  261.3 4.0 copy-start.17
  261.3 4.1 copy-start.12
  261.3 4.1 copy-start.21
  266.2 32.0 %copy-start.14 = (f32[9,8,128]{2,1,0:T(8,128)S(1)}, f32[9,8,128]{2,1,0:T(8,128)}, u32[]{:S(2)}) copy-start(f32[9,8,128]{2,1,0:T(8,128)} %get-tuple-element.441) | copy-start | bytes 110596
  268.2 26.0 %all-to-all-start.2 = ((f32[128,8,128]{2,1,0:T(8,128)}), f32[128,8,128]{2,1,0:T(8,128)S(1)}, u32[]{:S(2)}, u32[]{:S(2)}) async-start(f32[128,8,128]{2,1,0:T(8,128)} %bitcast.11), calls=%async_computation.2 | async-start | bytes 1048576 | tf_op jit(solution)/shard_map/all_to_all | solution.py:132
  276.3 281.4 %all-reduce.11.cloned.1.call-start = ((), (), s32[]{:S(2)}) async-start(), calls=%async_computation.4 | async-start | bytes 524288 | tf_op jit(solution)/shard_map/psum | solution.py:139
  277.0 282.3 %all-gather.3.cloned.1.call-start = ((), (), s32[]{:S(2)}) async-start(), calls=%async_computation.5 | async-start | bytes 2621440 | tf_op jit(solution)/shard_map/all_gather | solution.py:136
  299.3 26.9 %all-to-all-start.3 = ((f32[9,128,8]{0,2,1:T(8,128)}), f32[9,128,8]{0,2,1:T(8,128)S(1)}, u32[]{:S(2)}, u32[]{:S(2)}) async-start(f32[9,128,8]{0,2,1:T(8,128)} %bitcast.14), calls=%async_computation.3 | async-start | bytes 1048576 | tf_op jit(solution)/shard_map/all_to_all | solution.py:131
  (26 other events, 37.6 us)
Sparse Core Ops, SparseCore 0:
  282.7 274.9 all-reduce.10
Sparse Core Ops, SparseCore 1:
  298.3 29.1 all-gather.2
